TPU v7x, 32 devices: a whole 2x2x4 slice. The times are simulated.
32 devices in a mesh: groups: 2 (over x), ctx: 16 (over z, y, core).
Axes of the slice: x: 2, y: 2, z: 4, core: 2. Of those that a mesh axis runs over, the one named last changes fastest.
Arguments:
- queries: bfloat16 [4096, 2048], P(('groups', 'ctx')), parts along dimension 0, may hold values from -64 to 64
- keys: bfloat16 [4096, 512], P(('groups', 'ctx')), parts along dimension 0, may hold values from -6 to 6
- values: bfloat16 [4096, 512], P(('groups', 'ctx')), parts along dimension 0, may hold values from -6 to 6
- block_ids: int32 [4096], P(('groups', 'ctx')), parts along dimension 0, may hold values from 0 to 3, as said below
- out_weight: bfloat16 [2048, 2048], P('ctx'), may hold values from -0.59765625 to 0.59765625
- summary_gain: float32 [128], replicated, may hold values from 0.1 to 1.9
- norm_gain: float32 [2048], replicated, may hold values from 0.1 to 1.9
- routes: int32 [4096, 8], P(('groups', 'ctx')), parts along dimension 0, may hold values from 0 to 15, all different within a row; in each aligned block of 128 rows (0 to 127, 128 to 255, ...) at most 80 rows name the same one
- route_scores: float32 [4096, 8], P(('groups', 'ctx')), parts along dimension 0, may hold values from 0.02 to 1
- expert_gate: bfloat16 [16, 2048, 768], P('ctx'), may hold values from -0.125 to 0.125
- expert_up: bfloat16 [16, 2048, 768], P('ctx'), may hold values from -0.125 to 0.125
- expert_down: bfloat16 [16, 768, 2048], P('ctx'), may hold values from -0.21875 to 0.21875
Outputs:
- projected: bfloat16 [4096, 2048], P(('groups', 'ctx')), parts along dimension 0
- mixed: bfloat16 [4096, 2048], P(('groups', 'ctx')), parts along dimension 0
There are 2 independent parts, one for each index of `groups`. A program takes and returns all parts, laid end to end along the dimension named above; an argument that names none is the same for every part. Nothing has to cross between parts.
Inputs may be any that keep to these rules, and one draw needn't show every extreme that they name: `block_ids`: within each context shard's 128 tokens the block numbers never fall, start at 0 and take every value up to 3. `routes`: among the 128 tokens of one context shard no expert is chosen more than 80 times, and in every draw some expert is chosen exactly 80 times by some shard. A token's 8 experts differ.
All inputs are finite; a program needn't handle non-finite values.
Results may differ from a plain program's by a relative error of at most 0.0077.
Values may be sent and summed in bfloat16 or wider, within the bound.
A program may use at most 128 MiB of HBM per device.

v0:
```python
import math

import jax
import jax.numpy as jnp
from jax import lax
from jax.sharding import PartitionSpec as P

D = 2048
HQ = 16
KVH = 4
HD = 128
TOP = 8
EXP_DEV = 1
NB = 4


def normalize(x):
    return x * lax.rsqrt(jnp.mean(x * x, axis=-1, keepdims=True) + 1e-06)


def body(
    queries,
    keys,
    values,
    block_ids,
    out_weight,
    summary_gain,
    norm_gain,
    routes,
    route_scores,
    expert_gate,
    expert_up,
    expert_down,
):
    tokens_here = queries.shape[0]
    group = HQ // KVH
    scale = 1.0 / math.sqrt(HD)
    member = block_ids[None, :] == jnp.arange(NB, dtype=jnp.int32)[:, None]
    count = jnp.sum(member.astype(jnp.float32), axis=-1)
    indicator = member.astype(jnp.bfloat16)
    kmean = jnp.dot(indicator, keys, preferred_element_type=jnp.float32) / count[:, None]
    vmean = jnp.dot(indicator, values, preferred_element_type=jnp.float32) / count[:, None]
    summary_keys = (
        (normalize(kmean.reshape(NB, KVH, HD)) * summary_gain)
        .astype(jnp.bfloat16)
        .reshape(NB, KVH * HD)
    )
    summary_values = (
        normalize(vmean.reshape(NB, KVH, HD)).astype(jnp.bfloat16).reshape(NB, KVH * HD)
    )
    all_keys, all_values = (
        lax.all_gather(summary_keys, "ctx", axis=0, tiled=True),
        lax.all_gather(summary_values, "ctx", axis=0, tiled=True),
    )
    index = lax.axis_index("ctx")
    query = queries.reshape(tokens_here, KVH, group, HD)
    key_loc = keys.reshape(tokens_here, KVH, HD)
    remote_keys = all_keys.reshape(-1, KVH, HD)
    causal = jnp.arange(tokens_here)[:, None] >= jnp.arange(tokens_here)[None, :]
    owner = jnp.arange(remote_keys.shape[0], dtype=jnp.int32) // NB
    local = jnp.einsum("tkgd,skd->kgts", query, key_loc, preferred_element_type=jnp.float32) * scale
    local = jnp.where(causal[None, None], local, -jnp.inf)
    remote = (
        jnp.einsum("tkgd,skd->kgts", query, remote_keys, preferred_element_type=jnp.float32) * scale
    )
    remote = jnp.where((owner < index)[None, None, None, :], remote, -jnp.inf)
    scores = jnp.concatenate([local, remote], axis=-1)
    top = jnp.max(scores, axis=-1, keepdims=True)
    expo = jnp.exp(scores - top)
    weights = (expo / jnp.sum(expo, axis=-1, keepdims=True)).astype(jnp.bfloat16)
    every_value = jnp.concatenate(
        [values.reshape(tokens_here, KVH, HD), all_values.reshape(-1, KVH, HD)], axis=0
    )
    attended = jnp.einsum(
        "kgts,skd->tkgd", weights, every_value, preferred_element_type=jnp.float32
    )
    attended = attended.reshape(tokens_here, HQ * HD).astype(jnp.bfloat16)
    hidden = jnp.dot(
        attended,
        lax.all_gather(out_weight, "ctx", axis=0, tiled=True),
        preferred_element_type=jnp.float32,
    )
    normed = (normalize(hidden) * norm_gain).astype(jnp.bfloat16)
    combine = route_scores / jnp.sum(route_scores, axis=-1, keepdims=True)
    experts_all = EXP_DEV * lax.axis_size("ctx")
    capacity = max(2, 5 * tokens_here * TOP // (4 * experts_all))
    flat_routes = routes.reshape(-1)
    hits = (flat_routes[:, None] == jnp.arange(experts_all, dtype=jnp.int32)[None, :]).astype(
        jnp.int32
    )
    slot = jnp.sum(hits * (jnp.cumsum(hits, axis=0) - 1), axis=-1)
    target = flat_routes * capacity + slot
    source = jnp.arange(tokens_here * TOP, dtype=jnp.int32) // TOP
    outgoing = jnp.zeros((experts_all * capacity, D), jnp.bfloat16).at[target].set(normed[source])
    outgoing = outgoing.reshape(experts_all, capacity, D)
    arrived = lax.all_to_all(outgoing, "ctx", split_axis=0, concat_axis=0, tiled=True)
    senders = arrived.shape[0] // EXP_DEV
    width = arrived.shape[1]
    inputs = (
        arrived.reshape(senders, EXP_DEV, width, D)
        .transpose(1, 0, 2, 3)
        .reshape(EXP_DEV, senders * width, D)
    )
    gate = jnp.einsum("erd,edf->erf", inputs, expert_gate, preferred_element_type=jnp.float32)
    upper = jnp.einsum("erd,edf->erf", inputs, expert_up, preferred_element_type=jnp.float32)
    act = (jax.nn.silu(gate) * upper).astype(jnp.bfloat16)
    result = jnp.einsum(
        "erf,efd->erd", act, expert_down, preferred_element_type=jnp.float32
    ).astype(jnp.bfloat16)
    result = (
        result.reshape(EXP_DEV, senders, width, D)
        .transpose(1, 0, 2, 3)
        .reshape(senders * EXP_DEV, width, D)
    )
    returned = lax.all_to_all(result, "ctx", split_axis=0, concat_axis=0, tiled=True)
    returned = returned.reshape(experts_all * capacity, D)
    picked = jnp.take(returned, target, axis=0).reshape(tokens_here, TOP, D)
    blended = jnp.sum(combine[:, :, None] * picked.astype(jnp.float32), axis=1)
    return (hidden.astype(jnp.bfloat16), (hidden + blended).astype(jnp.bfloat16))


def solution(mesh):
    in_specs = (
        P(("groups", "ctx"), None),
        P(("groups", "ctx"), None),
        P(("groups", "ctx"), None),
        P(("groups", "ctx")),
        P("ctx", None),
        P(),
        P(),
        P(("groups", "ctx"), None),
        P(("groups", "ctx"), None),
        P("ctx", None, None),
        P("ctx", None, None),
        P("ctx", None, None),
    )
    out_specs = (P(("groups", "ctx"), None), P(("groups", "ctx"), None))
    return jax.shard_map(body, mesh=mesh, in_specs=in_specs, out_specs=out_specs, check_vma=False)
```

profile of v0, /device:TPU:13, one launch (start us, length us, event | category | flops | bytes accessed | tf_op | source)
XLA Modules:
  0.0 397.3 jit_solution(11848034568985104021)
XLA Ops:
  7.2 0.0 copy-start
  7.2 0.0 copy-start.4
  7.2 0.0 all-gather.4.cloned.1.call-start
  7.2 0.7 all-gather.4.cloned.1.call-update
  7.9 0.9 copy.81
  8.9 0.1 eq.42
  8.9 0.1 reshape.239
  9.0 0.9 reshape.236
  10.0 0.8 convert_reduce_fusion
  10.8 1.0 fusion.33
  11.8 0.1 reduce_sum.78
  11.9 0.7 broadcast_bitcast_fusion.2
  12.6 0.1 broadcast_bitcast_fusion
  12.7 16.0 %all-gather.1 = bf16[16,4,512]{2,1,0:T(4,128)(2,1)S(1)} all-gather(bf16[1,4,512]{2,1,0:T(4,128)(2,1)S(1)} %fusion.27), channel_id=1, replica_groups=mesh['groups'=2,'ctx'=16] {'ctx'}, dimensions={0}, use_global_device_ids=true | all-gather | bytes 69632 | tf_op jit(solution)/shard_map/all_gather | solution.py:52
  28.7 2.2 reshape.237
  30.9 1.0 copy.73
  31.9 1.0 fusion.36
  33.0 0.1 reduce_sum.77
  33.1 0.1 broadcast_bitcast_fusion.1
  33.2 22.5 %all-gather = bf16[16,4,512]{2,1,0:T(4,128)(2,1)S(1)} all-gather(bf16[1,4,512]{2,1,0:T(4,128)(2,1)S(1)} %fusion.26), channel_id=1, replica_groups=mesh['groups'=2,'ctx'=16] {'ctx'}, dimensions={0}, use_global_device_ids=true | all-gather | bytes 69632 | tf_op jit(solution)/shard_map/all_gather | solution.py:53
  55.7 0.7 reshape.235
  56.3 0.8 copy.75
  57.2 0.8 copy.74
  58.0 4.5 %reduce-window.6 = s32[16,8,128]{2,1,0:T(8,128)S(1)} reduce-window(s32[16,8,128]{2,1,0:T(8,128)S(1)} %fusion.22, s32[]{:T(128)} %constant.73.clone.1), window={size=1x1x128 pad=0_0x0_0x127_0}, to_apply=%region_7.8 | reduce-window | flops 2080768 | bytes 131076 | tf_op jit(solution)/shard_map/reduce-window
  62.5 0.1 slice.12
  62.5 0.1 copy.83
  62.7 0.1 copy.84
  62.8 0.0 copy-done.4
  62.8 0.6 broadcast_multiply_fusion
  63.4 0.8 copy.87
  64.2 0.7 mul.144
  64.9 0.0 copy-start.5
  64.9 0.0 copy-start.3
  64.9 1.4 fusion.35
  66.3 1.4 fusion.34
  67.7 0.1 add_add_fusion
  67.8 0.2 fusion.13
  68.1 0.0 copy-done.5
  68.1 0.0 copy-done.3
  68.1 1.3 convolution_convert_fusion.1
  69.4 16.0 %all-gather.4.cloned.1.call-done = bf16[2048,2048]{1,0:T(8,128)(2,1)} async-done(((bf16[128,2048]{1,0:T(8,128)(2,1)}), bf16[2048,2048]{1,0:T(8,128)(2,1)}) %all-gather.4.cloned.1.call-update) | async-done | bytes 8388624 | tf_op jit(solution)/shard_map/all_gather | solution.py:80
  85.4 4.9 %multiply_reduce_fusion.1 = (f32[128]{0:T(128)S(1)}, f32[128,2048]{1,0:T(8,128)S(1)}) fusion(bf16[128,2048]{0,1:T(8,128)(2,1)} %bitcast.86, bf16[2048,2048]{1,0:T(8,128)(2,1)} %all-gather.4.cloned.1.call-done), kind=kOutput, calls=%fused_computation.30 | convolution fusion | flops 1074265984 | bytes 9961984 | tf_op jit(solution)/shard_map/dot_general | solution.py:78
  90.3 0.0 copy-start.1
  90.3 1.0 copy-done.1
  91.3 0.0 copy-done.7
  91.3 1.0 multiply_convert_fusion
  92.2 24.0 %scatter_custom_fusion = bf16[1280,2048]{1,0:T(8,128)(2,1)} fusion(s32[1024]{0:T(1024)S(1)} %bitcast.93, bf16[128,2048]{1,0:T(8,128)(2,1)} %multiply_convert_fusion, s32[1024]{0:T(1024)S(1)} %broadcast_clamp_fusion.1, bf16[]{:T(256)} %constant.80.clone.1), kind=kCustom, calls=%fused_computation.6 | custom fusion | bytes 5243392 | tf_op jit(solution)/shard_map/scatter | solution.py:94
  116.3 120.1 %all_to_all.10 = bf16[16,80,2048]{2,1,0:T(8,128)(2,1)S(1)} all-to-all(bf16[16,80,2048]{2,1,0:T(8,128)(2,1)} %bitcast.82), channel_id=1, replica_groups=mesh['groups'=2,'ctx'=16] {'ctx'}, dimensions={0} | all-to-all | bytes 10485760 | tf_op jit(solution)/shard_map/all_to_all | solution.py:96
  236.4 0.0 copy-done.8
  236.4 4.3 %fusion.5 = f32[1280,768]{1,0:T(8,128)S(1)} fusion(bf16[1280,2048]{1,0:T(8,128)(2,1)S(1)} %bitcast.84, bf16[1,2048,768]{2,1,0:T(8,128)(2,1)S(1)} %copy-done.8), kind=kOutput, calls=%fused_computation.12 | convolution fusion | flops 4026531840 | bytes 12320768 | tf_op jit(solution)/shard_map/erd,edf->erf/dot_general | solution.py:104
  240.7 0.0 copy-done.9
  240.7 4.8 %fusion.2 = bf16[1280,768]{1,0:T(8,128)(2,1)S(1)} fusion(bf16[1280,2048]{1,0:T(8,128)(2,1)S(1)} %bitcast.85, f32[1280,768]{1,0:T(8,128)S(1)} %fusion.5, bf16[1,2048,768]{2,1,0:T(8,128)(2,1)S(1)} %copy-done.9), kind=kOutput, calls=%fused_computation.9 | convolution fusion | flops 4032430080 | bytes 14286848 | tf_op jit(solution)/shard_map/erd,edf->erf/dot_general | solution.py:105
  245.5 0.0 copy-done
  245.6 6.1 %convolution_convert_fusion = bf16[1280,2048]{1,0:T(8,128)(2,1)} fusion(bf16[1280,768]{1,0:T(8,128)(2,1)S(1)} %fusion.2, bf16[1,768,2048]{2,1,0:T(8,128)(2,1)S(1)} %copy-done), kind=kOutput, calls=%fused_computation.4 | convolution fusion | flops 4029153280 | bytes 10354688 | tf_op jit(solution)/shard_map/erf,efd->erd/dot_general | solution.py:107
  251.6 5.1 %all-to-all-start.1 = ((bf16[16,80,2048]{2,1,0:T(8,128)(2,1)}), bf16[16,80,2048]{2,1,0:T(8,128)(2,1)}, u32[]{:S(2)}, u32[]{:S(2)}) async-start(bf16[16,80,2048]{2,1,0:T(8,128)(2,1)} %bitcast.83), calls=%async_computation.1 | async-start | bytes 10485760 | tf_op jit(solution)/shard_map/all_to_all | solution.py:115
  256.7 0.1 reduce_sum.82
  256.8 0.1 copy.86
  257.0 0.0 copy-done.6
  257.0 0.1 copy.80
  257.1 114.5 %all-to-all-done.1 = bf16[16,80,2048]{2,1,0:T(8,128)(2,1)} async-done(((bf16[16,80,2048]{2,1,0:T(8,128)(2,1)}), bf16[16,80,2048]{2,1,0:T(8,128)(2,1)}, u32[]{:S(2)}, u32[]{:S(2)}) %all-to-all-start.1) | async-done | bytes 5242912 | tf_op jit(solution)/shard_map/all_to_all | solution.py:115
  371.6 12.0 %gather_fusion = bf16[1024,2048]{1,0:T(8,128)(2,1)} fusion(bf16[1280,2048]{1,0:T(8,128)(2,1)} %bitcast.23, s32[1024]{0:T(1024)S(1)} %broadcast_clamp_fusion), kind=kCustom, calls=%fused_computation.1 | custom fusion | bytes 8392704 | tf_op jit(solution)/shard_map/jit(_take)/gather | solution.py:117
  383.7 5.7 %multiply_reduce_fusion = f32[128,2048]{1,0:T(8,128)S(1)} fusion(bf16[1024,2048]{1,0:T(8,128)(2,1)} %gather_fusion, f32[128,8]{1,0:T(8,128)S(1)} %copy.80, pred[128,8]{1,0:T(8,128)(4,1)S(1)} %copy.86), kind=kLoop, calls=%fused_computation.3 | loop fusion | flops 8126464 | bytes 5248000 | tf_op jit(solution)/shard_map/reduce_sum | solution.py:118
  389.4 0.0 copy-done.2
  389.4 1.1 add_convert_fusion
  (28 shorter events, 0.3 us)
Async XLA Ops:
  7.2 238.4 %copy-start = (bf16[1,768,2048]{2,1,0:T(8,128)(2,1)S(1)}, bf16[1,768,2048]{2,1,0:T(8,128)(2,1)}, u32[]{:S(2)}) copy-start(bf16[1,768,2048]{2,1,0:T(8,128)(2,1)} %param.23) | copy-start | bytes 9437188
  7.2 55.6 %copy-start.4 = (s32[128,8]{0,1:T(8,128)S(1)}, s32[128,8]{0,1:T(8,128)}, u32[]{:S(2)}) copy-start(s32[128,8]{0,1:T(8,128)} %param.19) | copy-start | bytes 12292
  7.2 78.2 %all-gather.4.cloned.1.call-start = ((), (), s32[]{:S(2)}) async-start(), calls=%async_computation.2 | async-start | bytes 8912896 | tf_op jit(solution)/shard_map/all_gather | solution.py:80
  64.9 3.2 copy-start.5
  64.9 3.2 copy-start.3
  85.4 5.9 %copy-start.7 = (f32[2048]{0:T(1024)S(1)}, f32[2048]{0:T(1024)}, u32[]{:S(2)}) copy-start(f32[2048]{0:T(1024)} %param.18) | copy-start | bytes 24580
  90.3 1.0 copy-start.1
  116.3 120.1 %copy-start.8 = (bf16[1,2048,768]{2,1,0:T(8,128)(2,1)S(1)}, bf16[1,2048,768]{2,1,0:T(8,128)(2,1)}, u32[]{:S(2)}) copy-start(bf16[1,2048,768]{2,1,0:T(8,128)(2,1)} %param.21) | copy-start | bytes 9437188
  236.4 4.3 %copy-start.9 = (bf16[1,2048,768]{2,1,0:T(8,128)(2,1)S(1)}, bf16[1,2048,768]{2,1,0:T(8,128)(2,1)}, u32[]{:S(2)}) copy-start(bf16[1,2048,768]{2,1,0:T(8,128)(2,1)} %param.22) | copy-start | bytes 9437188
  251.6 5.4 %copy-start.6 = (f32[128,8]{0,1:T(8,128)S(1)}, f32[128,8]{0,1:T(8,128)}, u32[]{:S(2)}) copy-start(f32[128,8]{0,1:T(8,128)} %param.20) | copy-start | bytes 12292
  251.6 120.0 %all-to-all-start.1 = ((bf16[16,80,2048]{2,1,0:T(8,128)(2,1)}), bf16[16,80,2048]{2,1,0:T(8,128)(2,1)}, u32[]{:S(2)}, u32[]{:S(2)}) async-start(bf16[16,80,2048]{2,1,0:T(8,128)(2,1)} %bitcast.83), calls=%async_computation.1 | async-start | bytes 10485760 | tf_op jit(solution)/shard_map/all_to_all | solution.py:115
  383.7 5.7 %copy-start.2 = (f32[128,2048]{1,0:T(8,128)S(1)}, f32[128,2048]{1,0:T(8,128)}, u32[]{:S(2)}) copy-start(f32[128,2048]{1,0:T(8,128)} %copy-done.1) | copy-start | bytes 3145732
Sparse Core Ops, SparseCore 0:
  10.2 75.1 all-gather.3
where the time goes:
time: 398 us; the launch traced here: 397 us
  blocking collectives  159 us (40%)
  waiting for transfers between devices  131 us (33%)
  local copies, waits for them, and re-layouts  47.6 us (12%)
  matrix products  26.2 us (7%)
  other arithmetic  14.3 us (4%)
  between operations  14.3 us (4%)
  starting transfers between devices  5.11 us (1%)
    all_to_all x1, blocking collectives, body(): lax.all_to_all(outgoing, 'ctx', split_axis=0, concat_axis=0, tiled=True)  120 us
    all_to_all x1, waiting for transfers between devices, body(): lax.all_to_all(result, 'ctx', split_axis=0, concat_axis=0, tiled=True)  114 us
    scatter x1, local copies, waits for them, and re-layouts, body(): jnp.zeros((experts_all * capacity, D), jnp.bfloat16).at[target]  24 us
    all_gather x1, blocking collectives, body(): lax.all_gather(summary_values, 'ctx', axis=0, tiled=True)  22.5 us
    all_gather x1, blocking collectives, body(): lax.all_gather(summary_keys, 'ctx', axis=0, tiled=True)  16 us
    all_gather x1, waiting for transfers between devices, body(): lax.all_gather(out_weight, 'ctx', axis=0, tiled=True)  16 us
    gather x1, local copies, waits for them, and re-layouts, body(): picked = jnp.take(returned, target, axis=0).reshape(tokens_here, TOP, D)  12 us
  transfers between devices with their start and end apart: 2, of which 2 were waited for; matrix products, arithmetic and copies ran while one was open for 6% of the time, Pallas kernels for 0%

commit v1 on v0

--- a/solution.py
+++ b/solution.py
@@ -1,8 +1,11 @@
+import functools
 import math
 
 import jax
 import jax.numpy as jnp
 from jax import lax
+from jax.experimental import pallas as pl
+from jax.experimental.pallas import tpu as pltpu
 from jax.sharding import PartitionSpec as P
 
 D = 2048
@@ -16,6 +19,341 @@
 
 def normalize(x):
     return x * lax.rsqrt(jnp.mean(x * x, axis=-1, keepdims=True) + 1e-06)
+
+
+RING_BYTES = 16 * 2**20
+
+
+def chip_at(position, chips):
+    depth = chips // 2
+    y = position // depth
+    return (position * (1 - y) + (chips - 1 - position) * y) * 2 + y
+
+
+def moe_kernel(
+    n,
+    cap,
+    normed,
+    hidden,
+    share,
+    gate_hbm,
+    up_hbm,
+    down_hbm,
+    out,
+    gate_w,
+    up_w,
+    down_w,
+    tok,
+    wbuf,
+    rows_in,
+    act,
+    place,
+    comb,
+    mine,
+    outgo,
+    theirs,
+    ring_in,
+    load_sem,
+    own_sem,
+    w_send,
+    w_recv,
+    ag_send,
+    ag_recv,
+    pt_send,
+    pt_recv,
+    y_send,
+    y_recv,
+    rs_send_sem,
+    rs_recv_sem,
+):
+    tokens = normed.shape[0]
+    half = tokens // 2
+    width = normed.shape[1]
+    ff = gate_w.shape[1]
+    chips = n // 2
+    far = chips // 2
+    me = lax.axis_index("ctx")
+    core = me % 2
+    y = (me // 2) % 2
+    z = me // 4
+    pos = z * (1 - y) + (chips - 1 - z) * y
+    partner = me + 1 - 2 * core
+    ahead = chip_at((pos + 1) % chips, chips) * 2 + core
+    behind = chip_at((pos + chips - 1) % chips, chips) * 2 + core
+    neighbour = (ahead, behind)
+
+    loads = [
+        pltpu.make_async_copy(a, b, load_sem.at[k])
+        for k, (a, b) in enumerate(((gate_hbm, gate_w), (up_hbm, up_w), (down_hbm, down_w)))
+    ]
+    for load in loads:
+        load.start()
+    own = pltpu.make_async_copy(normed, tok.at[pos, core], own_sem)
+    own.start()
+
+    barrier = pltpu.get_barrier_semaphore()
+
+    def greet(k, _):
+        pl.semaphore_signal(barrier, inc=1, device_id={"ctx": (me + k) % n})
+        return 0
+
+    lax.fori_loop(1, n, greet, 0)
+    pl.semaphore_wait(barrier, n - 1)
+
+    def rows(h):
+        return pl.ds(h * half, half)
+
+    def chip(offset):
+        return (pos + offset + chips) % chips
+
+    def ag_copy(d, step, h):
+        sign = 1 - 2 * d
+        q = chip(-sign * (step - 1))
+        src = normed.at[rows(h)] if step == 1 else tok.at[q, core, rows(h)]
+        return pltpu.make_async_remote_copy(
+            src_ref=src,
+            dst_ref=tok.at[q, core, rows(h)],
+            send_sem=ag_send.at[d, step - 1, h],
+            recv_sem=ag_recv.at[d, step - 1, h],
+            device_id={"ctx": neighbour[d]},
+        )
+
+    def pt_copy(offset, h):
+        q = chip(offset)
+        src = normed.at[rows(h)] if offset == 0 else tok.at[q, core, rows(h)]
+        return pltpu.make_async_remote_copy(
+            src_ref=src,
+            dst_ref=tok.at[q, core, rows(h)],
+            send_sem=pt_send.at[offset % chips, h],
+            recv_sem=pt_recv.at[offset % chips, h],
+            device_id={"ctx": partner},
+        )
+
+    def order(d):
+        return (0, 1) if d == 0 else (1, 0)
+
+    for k in range(2):
+        for d in range(2):
+            ag_copy(d, 1, order(d)[k]).start()
+    for h in range(2):
+        pt_copy(0, h).start()
+
+    def w_copy(k):
+        target = (me + k) % n
+        return pltpu.make_async_remote_copy(
+            src_ref=share.at[target],
+            dst_ref=wbuf.at[pos * 2 + core],
+            send_sem=w_send.at[k],
+            recv_sem=w_recv.at[k],
+            device_id={"ctx": target},
+        )
+
+    def w_start(k, _):
+        w_copy(k).start()
+        return 0
+
+    def w_wait(k, _):
+        w_copy(k).wait()
+        return 0
+
+    lax.fori_loop(1, n, w_start, 0)
+    wbuf[pos * 2 + core] = share[me]
+    own.wait()
+    lax.fori_loop(1, n, w_wait, 0)
+    for load in loads:
+        load.wait()
+
+    def y_copy(offset):
+        q = chip(offset)
+        return pltpu.make_async_remote_copy(
+            src_ref=outgo.at[q],
+            dst_ref=theirs.at[q],
+            send_sem=y_send.at[offset % chips],
+            recv_sem=y_recv.at[offset % chips],
+            device_id={"ctx": partner},
+        )
+
+    def compute(offset):
+        q = chip(offset)
+        for h in range(2):
+            pt_copy(offset, h).wait_recv()
+        earlier = lax.broadcasted_iota(jnp.int32, (tokens, tokens), 0) < lax.broadcasted_iota(
+            jnp.int32, (tokens, tokens), 1
+        )
+        earlier = jnp.where(earlier, 1.0, 0.0).astype(jnp.bfloat16)
+        line = lax.broadcasted_iota(jnp.int32, (cap, tokens), 0).astype(jnp.float32)
+        for rel in range(2):
+            side = (core + rel) % 2
+            weight = wbuf[q * 2 + side]
+            chosen = jnp.where(weight > 0.0, 1.0, 0.0)
+            slot = jnp.dot(chosen.astype(jnp.bfloat16), earlier, preferred_element_type=jnp.float32)
+            slot = jnp.where(weight > 0.0, slot, -1.0)
+            hit = jnp.broadcast_to(slot[0:1], (cap, tokens)) == line
+            pick = jnp.where(hit, 1.0, 0.0).astype(jnp.bfloat16)
+            place[rel] = pick
+            scaled = jnp.where(hit, jnp.broadcast_to(weight[0:1], (cap, tokens)), 0.0)
+            comb[rel] = jnp.broadcast_to(jnp.sum(scaled, axis=1, keepdims=True), (cap, 128))
+            for c in range(0, width, 512):
+                rows_in[rel * cap : (rel + 1) * cap, c : c + 512] = jnp.dot(
+                    pick, tok[q, side, :, c : c + 512], preferred_element_type=jnp.float32
+                ).astype(jnp.bfloat16)
+
+        def in_tile(k, _):
+            cols = pl.ds(pl.multiple_of(k * 256, 256), 256)
+            x = rows_in[...]
+            g = jnp.dot(x, gate_w[:, cols], preferred_element_type=jnp.float32)
+            u = jnp.dot(x, up_w[:, cols], preferred_element_type=jnp.float32)
+            act[:, cols] = (g / (1.0 + jnp.exp(-g)) * u).astype(jnp.bfloat16)
+            return 0
+
+        lax.fori_loop(0, ff // 256, in_tile, 0)
+
+        def out_tile(k, _):
+            cols = pl.ds(pl.multiple_of(k * 512, 512), 512)
+            r = jnp.dot(act[...], down_w[:, cols], preferred_element_type=jnp.float32)
+            r = r.astype(jnp.bfloat16).astype(jnp.float32)
+            for rel, dest in ((0, mine), (1, outgo)):
+                part = r[rel * cap : (rel + 1) * cap] * comb[rel][:, 0:1]
+                dest[q, :, cols] = lax.dot_general(
+                    place[rel],
+                    part.astype(jnp.bfloat16),
+                    (((0,), (0,)), ((), ())),
+                    preferred_element_type=jnp.float32,
+                ).astype(jnp.bfloat16)
+            return 0
+
+        lax.fori_loop(0, width // 512, out_tile, 0)
+        y_copy(offset).start()
+
+    for step in range(1, far):
+        for k in range(2):
+            for d in range(2):
+                h = order(d)[k]
+                sign = 1 - 2 * d
+                ag_copy(d, step, h).wait_recv()
+                if step + 1 < far or k == 0:
+                    ag_copy(d, step + 1, h).start()
+                pt_copy(-sign * step, h).start()
+            if step == 1:
+                if k == 0:
+                    compute(0)
+            else:
+                compute((step - 1) * (2 * k - 1))
+    compute(1 - far)
+    compute(far - 1)
+    for d in range(2):
+        h = order(d)[0]
+        ag_copy(d, far, h).wait_recv()
+        pt_copy(far, h).start()
+
+    def sum_of(q, h):
+        return mine[q, rows(h)].astype(jnp.float32) + theirs[q, rows(h)].astype(jnp.float32)
+
+    def rs_copy(d, step, h, src):
+        return pltpu.make_async_remote_copy(
+            src_ref=src,
+            dst_ref=ring_in.at[d, step - 1, h],
+            send_sem=rs_send_sem.at[d, step - 1, h],
+            recv_sem=rs_recv_sem.at[d, step - 1, h],
+            device_id={"ctx": neighbour[d]},
+        )
+
+    def rs_step(d, step, k):
+        h = order(d)[k]
+        sign = 1 - 2 * d
+        q = chip(sign * (far + 1 - step))
+        if step == 1 or (step == 2 and k == 1):
+            mine[q, rows(h)] = sum_of(q, h).astype(jnp.bfloat16)
+            src = mine.at[q, rows(h)]
+        else:
+            src = ring_in.at[d, step - 2, h]
+            rs_copy(d, step - 1, h, src).wait_recv()
+            ring_in[d, step - 2, h] = (
+                ring_in[d, step - 2, h].astype(jnp.float32) + sum_of(q, h)
+            ).astype(jnp.bfloat16)
+        rs_copy(d, step, h, src).start()
+
+    for offset in range(chips):
+        if offset != far:
+            y_copy(offset).wait_recv()
+    for d in range(2):
+        rs_step(d, 2, 1)
+    compute(far)
+    y_copy(far).wait_recv()
+    sends = [(1, 0)]
+    for step in range(2, far + 1):
+        if step < far:
+            sends += [(step + 1, 1)]
+        sends += [(step, 0)]
+    for step, k in sends:
+        for d in range(2):
+            rs_step(d, step, k)
+    for h in range(2):
+        total = hidden[rows(h)] + sum_of(pos, h)
+        for d in range(2):
+            rs_copy(d, far, h, ring_in.at[d, far - 1, h]).wait_recv()
+            total = total + ring_in[d, far - 1, h].astype(jnp.float32)
+        out[rows(h)] = total.astype(jnp.bfloat16)
+
+    for d in range(2):
+        for step in range(1, far + 1):
+            for k in range(2):
+                h = order(d)[k]
+                if step < far or k == 0:
+                    ag_copy(d, step, h).wait_send()
+                if step > 1 or k == 0:
+                    rs_copy(d, step, h, ring_in.at[d, step - 1, h]).wait_send()
+    for offset in range(chips):
+        for h in range(2):
+            pt_copy(offset, h).wait_send()
+        y_copy(offset).wait_send()
+
+
+def moe_ring(normed, hidden, share, expert_gate, expert_up, expert_down, n, cap):
+    tokens, width = normed.shape
+    ff = expert_gate.shape[-1]
+    chips = n // 2
+    far = chips // 2
+    vmem = pl.BlockSpec(memory_space=pltpu.VMEM)
+    hbm = pl.BlockSpec(memory_space=pl.ANY)
+    dma = pltpu.SemaphoreType.DMA
+    bf16 = jnp.bfloat16
+    return pl.pallas_call(
+        functools.partial(moe_kernel, n, cap),
+        out_shape=jax.ShapeDtypeStruct((tokens, width), bf16),
+        in_specs=[vmem, vmem, vmem, hbm, hbm, hbm],
+        out_specs=vmem,
+        scratch_shapes=[
+            pltpu.VMEM((width, ff), bf16),
+            pltpu.VMEM((width, ff), bf16),
+            pltpu.VMEM((ff, width), bf16),
+            pltpu.VMEM((chips, 2, tokens, width), bf16),
+            pltpu.VMEM((n, 8, tokens), jnp.float32),
+            pltpu.VMEM((2 * cap, width), bf16),
+            pltpu.VMEM((2 * cap, ff), bf16),
+            pltpu.VMEM((2, cap, tokens), bf16),
+            pltpu.VMEM((2, cap, 128), jnp.float32),
+            pltpu.VMEM((chips, tokens, width), bf16),
+            pltpu.VMEM((chips, tokens, width), bf16),
+            pltpu.VMEM((chips, tokens, width), bf16),
+            pltpu.VMEM((2, far, 2, tokens // 2, width), bf16),
+            dma((3,)),
+            dma,
+            dma((n,)),
+            dma((n,)),
+            dma((2, far, 2)),
+            dma((2, far, 2)),
+            dma((chips, 2)),
+            dma((chips, 2)),
+            dma((chips,)),
+            dma((chips,)),
+            dma((2, far, 2)),
+            dma((2, far, 2)),
+        ],
+        compiler_params=pltpu.CompilerParams(
+            collective_id=1, has_side_effects=True, vmem_limit_bytes=60 * 2**20
+        ),
+    )(normed, hidden, share, expert_gate[0], expert_up[0], expert_down[0])
 
 
 def body(
@@ -48,10 +386,10 @@
     summary_values = (
         normalize(vmean.reshape(NB, KVH, HD)).astype(jnp.bfloat16).reshape(NB, KVH * HD)
     )
-    all_keys, all_values = (
-        lax.all_gather(summary_keys, "ctx", axis=0, tiled=True),
-        lax.all_gather(summary_values, "ctx", axis=0, tiled=True),
-    )
+    summaries = lax.all_gather(
+        jnp.concatenate([summary_keys, summary_values], axis=1), "ctx", axis=0, tiled=True
+    )
+    all_keys, all_values = summaries[:, : KVH * HD], summaries[:, KVH * HD :]
     index = lax.axis_index("ctx")
     query = queries.reshape(tokens_here, KVH, group, HD)
     key_loc = keys.reshape(tokens_here, KVH, HD)
@@ -84,6 +422,22 @@
     combine = route_scores / jnp.sum(route_scores, axis=-1, keepdims=True)
     experts_all = EXP_DEV * lax.axis_size("ctx")
     capacity = max(2, 5 * tokens_here * TOP // (4 * experts_all))
+    chips = experts_all // 2
+    if chips % 4 == 0 and experts_all * tokens_here * D * 2 <= RING_BYTES:
+        named = routes[:, :, None] == jnp.arange(experts_all, dtype=jnp.int32)[None, None, :]
+        share = jnp.sum(jnp.where(named, combine[:, :, None], 0.0), axis=1).T
+        share = jnp.broadcast_to(share[:, None, :], (experts_all, 8, tokens_here))
+        mixed = moe_ring(
+            normed,
+            hidden,
+            share,
+            expert_gate,
+            expert_up,
+            expert_down,
+            experts_all,
+            -(-capacity // 16) * 16,
+        )
+        return (hidden.astype(jnp.bfloat16), mixed)
     flat_routes = routes.reshape(-1)
     hits = (flat_routes[:, None] == jnp.arange(experts_all, dtype=jnp.int32)[None, :]).astype(
         jnp.int32

time: 398 us -> 206 us (0.52)
  the two profiles are of different devices: /device:TPU:13 before, /device:TPU:0 now
where the time goes in v1:
time: 206 us
  Pallas kernels  102 us (50%)
  waiting for transfers between devices  48.8 us (24%)
  blocking collectives  24.2 us (12%)
  between operations  14.2 us (7%)
  matrix products  7.99 us (4%)
  local copies, waits for them, and re-layouts  5.27 us (3%)
  other arithmetic  2.59 us (1%)
    pallas_call x1, Pallas kernels, moe_ring(): pl.pallas_call(functools.partial(moe_kernel, n, cap), out_shape=jax.Shape...  102 us
    all_gather x1, waiting for transfers between devices, body(): lax.all_gather(out_weight, 'ctx', axis=0, tiled=True)  48.1 us
    all_gather x1, blocking collectives, body(): lax.all_gather(jnp.concatenate([summary_keys, summary_values], axis=1), '...  24.2 us
    dot_general x1, matrix products, body(): jnp.dot(attended, lax.all_gather(out_weight, 'ctx', axis=0, tiled=True),...  4.76 us
  transfers between devices with their start and end apart: 1, of which 1 were waited for; matrix products, arithmetic and copies ran while one was open for 4% of the time, Pallas kernels for 0%

profile of v1, /device:TPU:0, one launch (start us, length us, event | category | flops | bytes accessed | tf_op | source)
XLA Modules:
  0.0 205.5 jit_solution(14204870031394267594)
XLA Ops:
  7.2 0.0 copy-start
  7.2 0.0 copy-start.2
  7.2 0.0 all-gather.3.cloned.1.call-start
  7.2 0.7 all-gather.3.cloned.1.call-update
  7.9 0.0 copy-start.3
  7.9 1.0 copy.37
  9.0 0.8 convert_reduce_fusion
  9.8 1.0 fusion.20
  10.8 0.9 reshape.96
  11.8 1.0 fusion.21
  12.8 0.1 reduce_sum.65
  12.9 0.1 reduce_sum.64
  13.0 0.0 copy-done
  13.0 0.1 broadcast_bitcast_fusion
  13.1 0.1 broadcast_bitcast_fusion.1
  13.2 24.2 %all-gather = bf16[16,4,1024]{2,1,0:T(4,128)(2,1)S(1)} all-gather(bf16[1,4,1024]{2,1,0:T(4,128)(2,1)S(1)} %maximum_bitcast_fusion.2), channel_id=1, replica_groups=mesh['groups'=2,'ctx'=16] {'ctx'}, dimensions={0}, use_global_device_ids=true | all-gather | bytes 139264 | tf_op jit(solution)/shard_map/all_gather | solution.py:389
  37.5 0.0 copy-done.2
  37.5 0.4 reshape.97
  37.9 0.0 copy-start.5
  37.9 0.1 copy.38
  38.0 0.0 copy-done.3
  38.1 0.3 fusion.23
  38.4 0.3 fusion.22
  38.8 0.0 copy-done.5
  38.8 0.2 fusion.5
  39.1 0.5 convolution_convert_fusion
  39.5 48.1 %all-gather.3.cloned.1.call-done = bf16[2048,2048]{1,0:T(8,128)(2,1)} async-done(((bf16[128,2048]{1,0:T(8,128)(2,1)}), bf16[2048,2048]{1,0:T(8,128)(2,1)}) %all-gather.3.cloned.1.call-update) | async-done | bytes 8388624 | tf_op jit(solution)/shard_map/all_gather | solution.py:418
  87.7 0.0 copy-start.4
  87.7 4.8 %multiply_reduce_fusion = (f32[128]{0:T(128)S(1)}, f32[128,2048]{1,0:T(8,128)S(1)}) fusion(bf16[128,2048]{0,1:T(8,128)(2,1)S(1)} %bitcast.51, bf16[2048,2048]{1,0:T(8,128)(2,1)} %all-gather.3.cloned.1.call-done), kind=kOutput, calls=%fused_computation.14 | convolution fusion | flops 1074265984 | bytes 9961984 | tf_op jit(solution)/shard_map/dot_general | solution.py:416
  92.4 0.0 copy-start.1
  92.4 0.0 copy-done.4
  92.5 1.3 multiply_convert_fusion
  93.7 0.6 broadcast_in_dim.44.share
  94.4 0.0 copy-done.1
  94.4 102.4 %shard_map.131 = bf16[128,2048]{1,0:T(8,128)(2,1)} custom-call(bf16[128,2048]{1,0:T(8,128)(2,1)} %get-tuple-element.2.normed, f32[128,2048]{1,0:T(8,128)} %copy-done.1, f32[16,8,128]{2,1,0:T(8,128)} %broadcast_in_dim.44.share, bf16[2048,768]{1,0:T(8,128)(2,1)} %bitcast.48, bf16[2048,768]{1,0:T(8,128)(2,1)} %bitcast.49, bf16[768,2048]{1,0:T(8,128)(2,1)} %bitcast.50), custom_call_target="tpu_custom_call" | custom-call | tf_op jit(solution)/shard_map/pallas_call | solution.py:321
  196.8 1.9 copy.75
  (18 shorter events, 0.2 us)
Async XLA Ops:
  7.2 5.8 %copy-start = (f32[128]{0:T(128)S(1)}, f32[128]{0:T(128)}, u32[]{:S(2)}) copy-start(f32[128]{0:T(128)} %param.17) | copy-start | bytes 1540
  7.2 30.3 %copy-start.2 = (bf16[128,2048]{1,0:T(8,128)(2,1)S(1)}, bf16[128,2048]{1,0:T(8,128)(2,1)}, u32[]{:S(2)}) copy-start(bf16[128,2048]{1,0:T(8,128)(2,1)} %param.12) | copy-start | bytes 1572868
  7.2 80.5 %all-gather.3.cloned.1.call-start = ((), (), s32[]{:S(2)}) async-start(), calls=%async_computation | async-start | bytes 8912896 | tf_op jit(solution)/shard_map/all_gather | solution.py:418
  7.9 30.1 %copy-start.3 = (f32[128,8]{0,1:T(8,128)S(1)}, f32[128,8]{0,1:T(8,128)}, u32[]{:S(2)}) copy-start(f32[128,8]{0,1:T(8,128)} %param.20) | copy-start | bytes 12292
  37.9 0.9 copy-start.5
  87.7 4.8 %copy-start.4 = (f32[2048]{0:T(1024)S(1)}, f32[2048]{0:T(1024)}, u32[]{:S(2)}) copy-start(f32[2048]{0:T(1024)} %param.18) | copy-start | bytes 24580
  92.4 1.9 copy-start.1
Sparse Core Ops, SparseCore 0:
  10.2 77.4 all-gather.2

commit v2 on v1

--- a/solution.py
+++ b/solution.py
@@ -30,16 +30,28 @@
     return (position * (1 - y) + (chips - 1 - position) * y) * 2 + y
 
 
-def moe_kernel(
+def layer_kernel(
     n,
     cap,
-    normed,
-    hidden,
+    queries,
+    keys,
+    values,
+    blocks,
+    weight_own,
+    key_gain,
+    norm_gain,
     share,
     gate_hbm,
     up_hbm,
     down_hbm,
+    projected,
     out,
+    normed,
+    hidden,
+    att,
+    wg,
+    sums_own,
+    sums,
     gate_w,
     up_w,
     down_w,
@@ -54,7 +66,14 @@
     theirs,
     ring_in,
     load_sem,
-    own_sem,
+    s_send,
+    s_recv,
+    wg_send,
+    wg_recv,
+    wx_send,
+    wx_recv,
+    wp_send,
+    wp_recv,
     w_send,
     w_recv,
     ag_send,
@@ -88,17 +107,57 @@
     ]
     for load in loads:
         load.start()
-    own = pltpu.make_async_copy(normed, tok.at[pos, core], own_sem)
-    own.start()
 
     barrier = pltpu.get_barrier_semaphore()
+    across = 1 - lax.axis_index("groups")
 
     def greet(k, _):
         pl.semaphore_signal(barrier, inc=1, device_id={"ctx": (me + k) % n})
         return 0
 
     lax.fori_loop(1, n, greet, 0)
-    pl.semaphore_wait(barrier, n - 1)
+    pl.semaphore_signal(barrier, inc=1, device_id={"groups": across})
+
+    def mean_of(ref):
+        ids = blocks[...]
+        member = jnp.where(
+            ids == lax.broadcasted_iota(jnp.int32, ids.shape, 0) % NB, 1.0, 0.0
+        )
+        count = jnp.sum(member, axis=1, keepdims=True)
+        return (
+            jnp.dot(member.astype(jnp.bfloat16), ref[...], preferred_element_type=jnp.float32)
+            / count
+        )
+
+    kmean, vmean = mean_of(keys), mean_of(values)
+    upper = lax.broadcasted_iota(jnp.int32, (2 * NB, HD), 0) < NB
+    for g in range(KVH):
+        cols = slice(g * HD, (g + 1) * HD)
+        sums_own[:, cols] = jnp.where(
+            upper, normalize(kmean[:, cols]) * key_gain[...], normalize(vmean[:, cols])
+        ).astype(jnp.bfloat16)
+    pl.semaphore_wait(barrier, n)
+
+    def s_copy(k):
+        target = (me + k) % n
+        return pltpu.make_async_remote_copy(
+            src_ref=sums_own,
+            dst_ref=sums.at[me],
+            send_sem=s_send.at[k],
+            recv_sem=s_recv.at[k],
+            device_id={"ctx": target},
+        )
+
+    def s_start(k, _):
+        s_copy(k).start()
+        return 0
+
+    def s_wait(k, _):
+        s_copy(k).wait()
+        return 0
+
+    lax.fori_loop(1, n, s_start, 0)
+    sums[me] = sums_own[...]
 
     def rows(h):
         return pl.ds(h * half, half)
@@ -132,33 +191,195 @@
     def order(d):
         return (0, 1) if d == 0 else (1, 0)
 
+    wrows = weight_own.shape[0]
+    side = 3 * wrows // 8
+    middle = wrows - 2 * side
+    group = 1 - across
+    mine_side = group * (side + middle)
+    other_side = across * (side + middle)
+
+    def w_rows(kind):
+        if kind == 0:
+            return mine_side, side
+        if kind == 1:
+            return side, middle
+        return other_side, side
+
+    def w_at(q, kind):
+        start, size = w_rows(kind)
+        return wg.at[q, pl.ds(core * wrows + start, size)]
+
+    def w_first(kind):
+        start, size = w_rows(kind)
+        return weight_own.at[pl.ds(start, size)]
+
+    def wg_copy(d, step, h):
+        sign = 1 - 2 * d
+        q = chip(-sign * (step - 1))
+        return pltpu.make_async_remote_copy(
+            src_ref=w_first(h) if step == 1 else w_at(q, h),
+            dst_ref=w_at(q, h),
+            send_sem=wg_send.at[d, step - 1, h],
+            recv_sem=wg_recv.at[d, step - 1, h],
+            device_id={"ctx": neighbour[d]},
+        )
+
+    def wx_copy(offset):
+        q = chip(offset)
+        return pltpu.make_async_remote_copy(
+            src_ref=w_at(q, 0),
+            dst_ref=w_at(q, 0),
+            send_sem=wx_send.at[offset % chips],
+            recv_sem=wx_recv.at[offset % chips],
+            device_id={"groups": across},
+        )
+
+    def wp_copy(offset, kind):
+        q = chip(offset)
+        return pltpu.make_async_remote_copy(
+            src_ref=w_first(kind) if offset == 0 else w_at(q, kind),
+            dst_ref=w_at(q, kind),
+            send_sem=wp_send.at[offset % chips, kind],
+            recv_sem=wp_recv.at[offset % chips, kind],
+            device_id={"ctx": partner},
+        )
+
+    for k in range(2):
+        for d in range(2):
+            wg_copy(d, 1, order(d)[k]).start()
+    for kind in range(3):
+        wp_copy(0, kind).start()
+    wg[pos, pl.ds(pl.multiple_of(core * wrows, wrows), wrows)] = weight_own[...]
+
+    def w_copy(k):
+        target = (me + k) % n
+        return pltpu.make_async_remote_copy(
+            src_ref=share.at[target],
+            dst_ref=wbuf.at[pos * 2 + core],
+            send_sem=w_send.at[k],
+            recv_sem=w_recv.at[k],
+            device_id={"ctx": target},
+        )
+
+    def w_start(k, _):
+        w_copy(k).start()
+        return 0
+
+    def w_wait(k, _):
+        w_copy(k).wait()
+        return 0
+
+    lax.fori_loop(1, n, w_start, 0)
+    wbuf[pos * 2 + core] = share[me]
+    lax.fori_loop(1, n, s_wait, 0)
+
+    many = HQ // KVH
+    scale = 1.0 / math.sqrt(HD)
+    tall = (many * tokens, tokens)
+    causal = lax.broadcasted_iota(jnp.int32, tall, 0) % tokens >= lax.broadcasted_iota(
+        jnp.int32, tall, 1
+    )
+    far_shape = (many * tokens, n * 2 * NB)
+    entry = lax.broadcasted_iota(jnp.int32, far_shape, 1)
+    seen = (entry % (2 * NB) < NB) & (entry // (2 * NB) < me)
+    contract_last = (((1,), (1,)), ((), ()))
+
+    def attend(g):
+        cols = slice(g * HD, (g + 1) * HD)
+        heads = [slice((g * many + i) * HD, (g * many + i + 1) * HD) for i in range(many)]
+        q = jnp.concatenate([queries[:, c] for c in heads], axis=0)
+        table = sums[:, :, cols].astype(jnp.float32).reshape(n * 2 * NB, HD)
+        shifted = jnp.concatenate([table[NB:], table[:NB]], axis=0).astype(jnp.bfloat16)
+        table = table.astype(jnp.bfloat16)
+        near = (
+            lax.dot_general(q, keys[:, cols], contract_last, preferred_element_type=jnp.float32)
+            * scale
+        )
+        near = jnp.where(causal, near, -jnp.inf)
+        remote = lax.dot_general(q, table, contract_last, preferred_element_type=jnp.float32) * scale
+        remote = jnp.where(seen, remote, -jnp.inf)
+        top = jnp.maximum(
+            jnp.max(near, axis=1, keepdims=True), jnp.max(remote, axis=1, keepdims=True)
+        )
+        near, remote = jnp.exp(near - top), jnp.exp(remote - top)
+        total = jnp.sum(near, axis=1, keepdims=True) + jnp.sum(remote, axis=1, keepdims=True)
+        near, remote = (near / total).astype(jnp.bfloat16), (remote / total).astype(jnp.bfloat16)
+        result = jnp.dot(
+            near, values[:, cols], preferred_element_type=jnp.float32
+        ) + jnp.dot(remote, shifted, preferred_element_type=jnp.float32)
+        result = result.astype(jnp.bfloat16)
+        for i, c in enumerate(heads):
+            att[:, c] = result[i * tokens : (i + 1) * tokens]
+
+    def project(offset):
+        q = chip(offset)
+        for kind in range(3):
+            wp_copy(offset, kind).wait_recv()
+        place_at = pl.multiple_of(chip_at(q, chips) * 2 * wrows, 2 * wrows)
+        left = att[:, pl.ds(place_at, 2 * wrows)]
+
+        def tile(k, _):
+            cols = pl.ds(pl.multiple_of(k * 512, 512), 512)
+            part = jnp.dot(left, wg[q, :, cols], preferred_element_type=jnp.float32)
+            hidden[:, cols] = part if offset == 0 else hidden[:, cols] + part
+            return 0
+
+        lax.fori_loop(0, width // 512, tile, 0)
+
+    def w_step(step, k):
+        for d in range(2):
+            h = order(d)[k]
+            sign = 1 - 2 * d
+            wg_copy(d, step, h).wait_recv()
+            if step + 1 < far or (step + 1 == far and k == 0):
+                wg_copy(d, step + 1, h).start()
+            if h == 0:
+                wx_copy(-sign * step).start()
+            wp_copy(-sign * step, h).start()
+
+    def x_step(offset):
+        wx_copy(offset).wait_recv()
+        wp_copy(offset, 2).start()
+
+    attend(0)
+    attend(1)
+    w_step(1, 0)
+    attend(2)
+    w_step(1, 1)
+    attend(3)
+    for step in range(2, far):
+        w_step(step, 0)
+        x_step(1 - step)
+        x_step(step - 1)
+        if step == 2:
+            project(0)
+        else:
+            project(2 - step)
+        w_step(step, 1)
+        if step > 2:
+            project(step - 2)
+    w_step(far, 0)
+    x_step(1 - far)
+    x_step(far - 1)
+    project(2 - far)
+    project(far - 2)
+    x_step(far)
+    project(1 - far)
+    project(far - 1)
+    project(far)
+    for h in range(2):
+        hid = hidden[rows(h)]
+        projected[rows(h)] = hid.astype(jnp.bfloat16)
+        tidy = (normalize(hid) * norm_gain[...]).astype(jnp.bfloat16)
+        normed[rows(h)] = tidy
+        tok[pos, core, rows(h)] = tidy
+
     for k in range(2):
         for d in range(2):
             ag_copy(d, 1, order(d)[k]).start()
     for h in range(2):
         pt_copy(0, h).start()
 
-    def w_copy(k):
-        target = (me + k) % n
-        return pltpu.make_async_remote_copy(
-            src_ref=share.at[target],
-            dst_ref=wbuf.at[pos * 2 + core],
-            send_sem=w_send.at[k],
-            recv_sem=w_recv.at[k],
-            device_id={"ctx": target},
-        )
-
-    def w_start(k, _):
-        w_copy(k).start()
-        return 0
-
-    def w_wait(k, _):
-        w_copy(k).wait()
-        return 0
-
-    lax.fori_loop(1, n, w_start, 0)
-    wbuf[pos * 2 + core] = share[me]
-    own.wait()
     lax.fori_loop(1, n, w_wait, 0)
     for load in loads:
         load.wait()
@@ -309,36 +530,76 @@
         y_copy(offset).wait_send()
 
 
-def moe_ring(normed, hidden, share, expert_gate, expert_up, expert_down, n, cap):
-    tokens, width = normed.shape
+    for d in range(2):
+        for step in range(1, far + 1):
+            for k in range(2):
+                if step < far or k == 0:
+                    wg_copy(d, step, order(d)[k]).wait_send()
+    for offset in range(chips):
+        if offset > 0:
+            wx_copy(offset).wait_send()
+        for kind in range(3):
+            wp_copy(offset, kind).wait_send()
+
+
+def layer_ring(
+    queries,
+    keys,
+    values,
+    block_ids,
+    out_weight,
+    summary_gain,
+    norm_gain,
+    share,
+    expert_gate,
+    expert_up,
+    expert_down,
+    n,
+    cap,
+):
+    tokens, width = queries.shape
     ff = expert_gate.shape[-1]
     chips = n // 2
     far = chips // 2
     vmem = pl.BlockSpec(memory_space=pltpu.VMEM)
     hbm = pl.BlockSpec(memory_space=pl.ANY)
     dma = pltpu.SemaphoreType.DMA
-    bf16 = jnp.bfloat16
+    bf16, f32 = jnp.bfloat16, jnp.float32
+    result = jax.ShapeDtypeStruct((tokens, width), bf16)
     return pl.pallas_call(
-        functools.partial(moe_kernel, n, cap),
-        out_shape=jax.ShapeDtypeStruct((tokens, width), bf16),
-        in_specs=[vmem, vmem, vmem, hbm, hbm, hbm],
-        out_specs=vmem,
+        functools.partial(layer_kernel, n, cap),
+        out_shape=(result, result),
+        in_specs=[vmem] * 8 + [hbm] * 3,
+        out_specs=(vmem, vmem),
         scratch_shapes=[
+            pltpu.VMEM((tokens, width), bf16),
+            pltpu.VMEM((tokens, width), f32),
+            pltpu.VMEM((tokens, width), bf16),
+            pltpu.VMEM((chips, 2 * out_weight.shape[0], width), bf16),
+            pltpu.VMEM((2 * NB, KVH * HD), bf16),
+            pltpu.VMEM((n, 2 * NB, KVH * HD), bf16),
             pltpu.VMEM((width, ff), bf16),
             pltpu.VMEM((width, ff), bf16),
             pltpu.VMEM((ff, width), bf16),
             pltpu.VMEM((chips, 2, tokens, width), bf16),
-            pltpu.VMEM((n, 8, tokens), jnp.float32),
+            pltpu.VMEM((n, 8, tokens), f32),
             pltpu.VMEM((2 * cap, width), bf16),
             pltpu.VMEM((2 * cap, ff), bf16),
             pltpu.VMEM((2, cap, tokens), bf16),
-            pltpu.VMEM((2, cap, 128), jnp.float32),
+            pltpu.VMEM((2, cap, 128), f32),
             pltpu.VMEM((chips, tokens, width), bf16),
             pltpu.VMEM((chips, tokens, width), bf16),
             pltpu.VMEM((chips, tokens, width), bf16),
             pltpu.VMEM((2, far, 2, tokens // 2, width), bf16),
             dma((3,)),
-            dma,
+            dma((n,)),
+            dma((n,)),
+            dma((2, far, 2)),
+            dma((2, far, 2)),
+            dma((chips,)),
+            dma((chips,)),
+            dma((chips, 3)),
+            dma((chips, 3)),
             dma((n,)),
             dma((n,)),
             dma((2, far, 2)),
@@ -351,9 +612,21 @@
             dma((2, far, 2)),
         ],
         compiler_params=pltpu.CompilerParams(
-            collective_id=1, has_side_effects=True, vmem_limit_bytes=60 * 2**20
+            collective_id=1, has_side_effects=True, vmem_limit_bytes=62 * 2**20
         ),
-    )(normed, hidden, share, expert_gate[0], expert_up[0], expert_down[0])
+    )(
+        queries,
+        keys,
+        values,
+        jnp.broadcast_to(block_ids[None, :], (2 * NB, tokens)),
+        out_weight,
+        summary_gain[None, :],
+        norm_gain[None, :],
+        share,
+        expert_gate[0],
+        expert_up[0],
+        expert_down[0],
+    )
 
 
 def body(
@@ -371,6 +644,30 @@
     expert_down,
 ):
     tokens_here = queries.shape[0]
+    combine = route_scores / jnp.sum(route_scores, axis=-1, keepdims=True)
+    experts_all = EXP_DEV * lax.axis_size("ctx")
+    capacity = max(2, 5 * tokens_here * TOP // (4 * experts_all))
+    chips = experts_all // 2
+    fits = experts_all * tokens_here * D * 2 <= RING_BYTES
+    if fits and chips % 4 == 0 and lax.axis_size("groups") == 2:
+        named = routes[:, :, None] == jnp.arange(experts_all, dtype=jnp.int32)[None, None, :]
+        share = jnp.sum(jnp.where(named, combine[:, :, None], 0.0), axis=1).T
+        share = jnp.broadcast_to(share[:, None, :], (experts_all, 8, tokens_here))
+        return layer_ring(
+            queries,
+            keys,
+            values,
+            block_ids,
+            out_weight,
+            summary_gain,
+            norm_gain,
+            share,
+            expert_gate,
+            expert_up,
+            expert_down,
+            experts_all,
+            -(-capacity // 16) * 16,
+        )
     group = HQ // KVH
     scale = 1.0 / math.sqrt(HD)
     member = block_ids[None, :] == jnp.arange(NB, dtype=jnp.int32)[:, None]
@@ -419,25 +716,6 @@
         preferred_element_type=jnp.float32,
     )
     normed = (normalize(hidden) * norm_gain).astype(jnp.bfloat16)
-    combine = route_scores / jnp.sum(route_scores, axis=-1, keepdims=True)
-    experts_all = EXP_DEV * lax.axis_size("ctx")
-    capacity = max(2, 5 * tokens_here * TOP // (4 * experts_all))
-    chips = experts_all // 2
-    if chips % 4 == 0 and experts_all * tokens_here * D * 2 <= RING_BYTES:
-        named = routes[:, :, None] == jnp.arange(experts_all, dtype=jnp.int32)[None, None, :]
-        share = jnp.sum(jnp.where(named, combine[:, :, None], 0.0), axis=1).T
-        share = jnp.broadcast_to(share[:, None, :], (experts_all, 8, tokens_here))
-        mixed = moe_ring(
-            normed,
-            hidden,
-            share,
-            expert_gate,
-            expert_up,
-            expert_down,
-            experts_all,
-            -(-capacity // 16) * 16,
-        )
-        return (hidden.astype(jnp.bfloat16), mixed)
     flat_routes = routes.reshape(-1)
     hits = (flat_routes[:, None] == jnp.arange(experts_all, dtype=jnp.int32)[None, :]).astype(
         jnp.int32

time: 206 us -> 154 us (0.75)
  waiting for transfers between devices: 48.8 us -> 0 us
  Pallas kernels: 102 us -> 145 us
  blocking collectives: 24.2 us -> 0 us
  between operations: 14.2 us -> 0.64 us
  matrix products: 7.99 us -> 0 us
    all_gather x1 -> x0, waiting for transfers between devices: 48.1 us -> none  [body(): lax.all_gather(out_weight, 'ctx', axis=0, tiled=True)]
    pallas_call x1, Pallas kernels: 102 us -> 145 us  [layer_ring(): pl.pallas_call(functools.partial(layer_kernel, n, cap), out_shape=(result...]
    all_gather x1 -> x0, blocking collectives: 24.2 us -> none  [body(): lax.all_gather(jnp.concatenate([summary_keys, summary_values], axis=1), '...]
    dot_general x6 -> x0, matrix products: 7.99 us -> none  [the longest x1 4.76 us: body(): jnp.dot(attended, lax.all_gather(out_weight, 'ctx', axis=0, tiled=True),...]
  transfers between devices with their start and end apart: 1 -> 0, of which waited for: 1 -> 0; matrix products, arithmetic and copies ran while one was open for 4% -> 0% of each run, Pallas kernels for 0% -> 0%
where the time goes in v2:
time: 154 us; the launch traced here: 153 us
  Pallas kernels  145 us (94%)
  local copies, waits for them, and re-layouts  5.65 us (4%)
  other arithmetic  2.1 us (1%)
    pallas_call x1, Pallas kernels, layer_ring(): pl.pallas_call(functools.partial(layer_kernel, n, cap), out_shape=(result...  145 us
    unnamed x2, local copies, waits for them, and re-layouts  3.76 us

profile of v2, /device:TPU:0, one launch (start us, length us, event | category | flops | bytes accessed | tf_op | source)
XLA Modules:
  0.0 153.4 jit_solution(12039812278338176760)
XLA Ops:
  0.6 0.7 reduce_sum.18
  1.3 0.7 broadcast_divide_fusion
  2.0 0.7 select_reduce_fusion
  2.7 1.3 broadcast_in_dim.20.blocks
  4.0 0.6 broadcast_in_dim.39.share
  4.6 145.0 %shard_map.131 = (bf16[128,2048]{1,0:T(8,128)(2,1)}, bf16[128,2048]{1,0:T(8,128)(2,1)}) custom-call(bf16[128,2048]{1,0:T(8,128)(2,1)} %queries.1, bf16[128,512]{1,0:T(8,128)(2,1)} %keys.1, bf16[128,512]{1,0:T(8,128)(2,1)} %values.1, s32[8,128]{1,0:T(8,128)} %broadcast_in_dim.20.blocks, bf16[128,2048]{1,0:T(8,128)(2,1)} %weight_own.1, f32[1,128]{1,0:T(1,128)} %bitcast.11, ...), custom_call_target="tpu_custom_call" | custom-call | tf_op jit(solution)/shard_map/pallas_call | solution.py:569
  149.6 1.9 %copy.18 = bf16[128,2048]{1,0:T(8,128)(2,1)} copy(bf16[128,2048]{1,0:T(8,128)(2,1)} %get-tuple-element.4) | data formatting | bytes 1048576
  151.5 1.9 %copy.19 = bf16[128,2048]{1,0:T(8,128)(2,1)} copy(bf16[128,2048]{1,0:T(8,128)(2,1)} %get-tuple-element.5) | data formatting | bytes 1048576

commit v3 on v2

--- a/solution.py
+++ b/solution.py
@@ -40,7 +40,8 @@
     weight_own,
     key_gain,
     norm_gain,
-    share,
+    routes,
+    route_scores,
     gate_hbm,
     up_hbm,
     down_hbm,
@@ -52,6 +53,7 @@
     wg,
     sums_own,
     sums,
+    share,
     gate_w,
     up_w,
     down_w,
@@ -119,10 +121,9 @@
     pl.semaphore_signal(barrier, inc=1, device_id={"groups": across})
 
     def mean_of(ref):
-        ids = blocks[...]
-        member = jnp.where(
-            ids == lax.broadcasted_iota(jnp.int32, ids.shape, 0) % NB, 1.0, 0.0
-        )
+        shape = (2 * NB, tokens)
+        ids = jnp.broadcast_to(blocks[...], shape)
+        member = jnp.where(ids == lax.broadcasted_iota(jnp.int32, shape, 0) % NB, 1.0, 0.0)
         count = jnp.sum(member, axis=1, keepdims=True)
         return (
             jnp.dot(member.astype(jnp.bfloat16), ref[...], preferred_element_type=jnp.float32)
@@ -269,6 +270,14 @@
         w_copy(k).wait()
         return 0
 
+    chosen_scores = route_scores[...]
+    combine = chosen_scores / jnp.sum(chosen_scores, axis=0, keepdims=True)
+    expert = lax.broadcasted_iota(jnp.int32, (n, tokens), 0)
+    table_of = jnp.zeros((n, tokens), jnp.float32)
+    for c in range(TOP):
+        table_of = table_of + jnp.where(routes[c : c + 1] == expert, combine[c : c + 1], 0.0)
+    for e in range(n):
+        share[e] = jnp.broadcast_to(table_of[e : e + 1], (8, tokens))
     lax.fori_loop(1, n, w_start, 0)
     wbuf[pos * 2 + core] = share[me]
     lax.fori_loop(1, n, s_wait, 0)
@@ -542,6 +551,16 @@
             wp_copy(offset, kind).wait_send()
 
 
+def write_kernel(a, b, a_out, b_out, sem):
+    copies = [
+        pltpu.make_async_copy(x, y, sem.at[k]) for k, (x, y) in enumerate(((a, a_out), (b, b_out)))
+    ]
+    for copy in copies:
+        copy.start()
+    for copy in copies:
+        copy.wait()
+
+
 def layer_ring(
     queries,
     keys,
@@ -550,7 +569,8 @@
     out_weight,
     summary_gain,
     norm_gain,
-    share,
+    routes,
+    route_scores,
     expert_gate,
     expert_up,
     expert_down,
@@ -566,10 +586,10 @@
     dma = pltpu.SemaphoreType.DMA
     bf16, f32 = jnp.bfloat16, jnp.float32
     result = jax.ShapeDtypeStruct((tokens, width), bf16)
-    return pl.pallas_call(
+    pair = pl.pallas_call(
         functools.partial(layer_kernel, n, cap),
         out_shape=(result, result),
-        in_specs=[vmem] * 8 + [hbm] * 3,
+        in_specs=[vmem] * 9 + [hbm] * 3,
         out_specs=(vmem, vmem),
         scratch_shapes=[
             pltpu.VMEM((tokens, width), bf16),
@@ -578,6 +598,7 @@
             pltpu.VMEM((chips, 2 * out_weight.shape[0], width), bf16),
             pltpu.VMEM((2 * NB, KVH * HD), bf16),
             pltpu.VMEM((n, 2 * NB, KVH * HD), bf16),
+            pltpu.VMEM((n, 8, tokens), f32),
             pltpu.VMEM((width, ff), bf16),
             pltpu.VMEM((width, ff), bf16),
             pltpu.VMEM((ff, width), bf16),
@@ -618,15 +639,23 @@
         queries,
         keys,
         values,
-        jnp.broadcast_to(block_ids[None, :], (2 * NB, tokens)),
+        block_ids[None, :],
         out_weight,
         summary_gain[None, :],
         norm_gain[None, :],
-        share,
+        routes.T,
+        route_scores.T,
         expert_gate[0],
         expert_up[0],
         expert_down[0],
     )
+    return pl.pallas_call(
+        write_kernel,
+        out_shape=(result, result),
+        in_specs=[vmem] * 2,
+        out_specs=(hbm, hbm),
+        scratch_shapes=[dma((2,))],
+    )(*pair)
 
 
 def body(
@@ -650,9 +679,6 @@
     chips = experts_all // 2
     fits = experts_all * tokens_here * D * 2 <= RING_BYTES
     if fits and chips % 4 == 0 and lax.axis_size("groups") == 2:
-        named = routes[:, :, None] == jnp.arange(experts_all, dtype=jnp.int32)[None, None, :]
-        share = jnp.sum(jnp.where(named, combine[:, :, None], 0.0), axis=1).T
-        share = jnp.broadcast_to(share[:, None, :], (experts_all, 8, tokens_here))
         return layer_ring(
             queries,
             keys,
@@ -661,7 +687,8 @@
             out_weight,
             summary_gain,
             norm_gain,
-            share,
+            routes,
+            route_scores,
             expert_gate,
             expert_up,
             expert_down,

time: 154 us -> 148 us (0.961)
  local copies, waits for them, and re-layouts: 5.65 us -> 0 us
  other arithmetic: 2.1 us -> 0 us
  Pallas kernels: 145 us -> 147 us
    unnamed x2 -> x0, local copies, waits for them, and re-layouts: 3.76 us -> none
    pallas_call x0 -> x1, Pallas kernels: none -> 2.18 us  [layer_ring(): pl.pallas_call(write_kernel, out_shape=(result, result), in_specs=[vmem]...]
    broadcast_in_dim x2 -> x0, local copies, waits for them, and re-layouts: 1.88 us -> none  [the longest x1 1.25 us: layer_ring(): jnp.broadcast_to(block_ids[None, :], (2 * NB, tokens))]
where the time goes in v3:
time: 148 us
  Pallas kernels  147 us (99%)
    pallas_call x1, Pallas kernels, layer_ring(): pl.pallas_call(functools.partial(layer_kernel, n, cap), out_shape=(result...  145 us

profile of v3, /device:TPU:0, one launch (start us, length us, event | category | flops | bytes accessed | tf_op | source)
XLA Modules:
  0.0 148.1 jit_solution(2000977148085611547)
XLA Ops:
  0.6 145.1 %shard_map.131 = (bf16[128,2048]{1,0:T(8,128)(2,1)}, bf16[128,2048]{1,0:T(8,128)(2,1)}) custom-call(bf16[128,2048]{1,0:T(8,128)(2,1)} %queries.1, bf16[128,512]{1,0:T(8,128)(2,1)} %keys.1, bf16[128,512]{1,0:T(8,128)(2,1)} %values.1, s32[1,128]{1,0:T(1,128)} %bitcast.14, bf16[128,2048]{1,0:T(8,128)(2,1)} %weight_own.1, f32[1,128]{1,0:T(1,128)} %bitcast.15, ...), custom_call_target="tpu_custom_call" | custom-call | tf_op jit(solution)/shard_map/pallas_call | solution.py:589
  145.7 2.2 %shard_map.132 = (bf16[128,2048]{1,0:T(8,128)(2,1)}, bf16[128,2048]{1,0:T(8,128)(2,1)}) custom-call(bf16[128,2048]{1,0:T(8,128)(2,1)} %get-tuple-element.4.a, bf16[128,2048]{1,0:T(8,128)(2,1)} %get-tuple-element.5.b), custom_call_target="tpu_custom_call" | custom-call | tf_op jit(solution)/shard_map/pallas_call | solution.py:652

commit v4 on v3

--- a/solution.py
+++ b/solution.py
@@ -193,7 +193,7 @@
         return (0, 1) if d == 0 else (1, 0)
 
     wrows = weight_own.shape[0]
-    side = 3 * wrows // 8
+    side = wrows // 4
     middle = wrows - 2 * side
     group = 1 - across
     mine_side = group * (side + middle)

time: 148 us -> 147 us (level)
  no operation moved by 1% of the time
where the time goes in v4:
time: 147 us
  Pallas kernels  146 us (99%)
    pallas_call x1, Pallas kernels, layer_ring(): pl.pallas_call(functools.partial(layer_kernel, n, cap), out_shape=(result...  144 us

profile of v4, /device:TPU:0, one launch (start us, length us, event | category | flops | bytes accessed | tf_op | source)
XLA Modules:
  0.0 147.0 jit_solution(8379476434412805162)
XLA Ops:
  0.6 144.0 %shard_map.131 = (bf16[128,2048]{1,0:T(8,128)(2,1)}, bf16[128,2048]{1,0:T(8,128)(2,1)}) custom-call(bf16[128,2048]{1,0:T(8,128)(2,1)} %queries.1, bf16[128,512]{1,0:T(8,128)(2,1)} %keys.1, bf16[128,512]{1,0:T(8,128)(2,1)} %values.1, s32[1,128]{1,0:T(1,128)} %bitcast.14, bf16[128,2048]{1,0:T(8,128)(2,1)} %weight_own.1, f32[1,128]{1,0:T(1,128)} %bitcast.15, ...), custom_call_target="tpu_custom_call" | custom-call | tf_op jit(solution)/shard_map/pallas_call | solution.py:589
  144.6 2.2 %shard_map.132 = (bf16[128,2048]{1,0:T(8,128)(2,1)}, bf16[128,2048]{1,0:T(8,128)(2,1)}) custom-call(bf16[128,2048]{1,0:T(8,128)(2,1)} %get-tuple-element.4.a, bf16[128,2048]{1,0:T(8,128)(2,1)} %get-tuple-element.5.b), custom_call_target="tpu_custom_call" | custom-call | tf_op jit(solution)/shard_map/pallas_call | solution.py:652
